TPU v7x, 32 devices: a whole 2x2x4 slice. The times are simulated.
32 devices in a mesh: mem: 8 (over z, core), dom: 4 (over y, x).
Axes of the slice: x: 2, y: 2, z: 4, core: 2. Of those that a mesh axis runs over, the one named last changes fastest.
Arguments:
- prior_ensemble: float32 [64, 4, 512, 512], P('mem', None, 'dom'), may hold values from -6 to 6
- spreading_factor: float32 [4], replicated, may hold values from 0.05 to 0.24
- tendency_matrix: float32 [4, 4], replicated, may hold values from -0.6 to 0.6
- measured_data: float32 [4, 4096], P('dom', 'mem'), may hold values from -6 to 6
- inverse_error: float32 [4, 4096], P('dom', 'mem'), may hold values from 0.1 to 1
- assigned_subregion: int32 [4, 4096, 1], P('dom', 'mem'), may hold values from 0 to 31; in each aligned block of 512 rows (0 to 511, 512 to 1023, ..., all dimensions but the last counted through in order) at most 32 rows name the same one
- measured_entry: int32 [4, 4096], P('dom', 'mem'), may hold values from 0 to 8191
- taper_index: int32 [4, 4096], P('dom', 'mem'), may hold values from 0 to 63
- taper_factors: float32 [64], replicated, may hold values from 0.2 to 1
Outputs:
- analysis: float32 [64, 4, 512, 512], P('mem', None, 'dom')
Inputs may be any that keep to these rules, and one draw needn't show every extreme that they name: `assigned_subregion`: in the rows of one device no patch is named by more than 32 rows, a bound that some block reaches.
All inputs are finite; a program needn't handle non-finite values.
Results may differ from a plain program's by a relative error of at most 0.0003.
Values sent between devices are 32-bit elements; how exact they have to be, the bound alone decides.
A program may use at most 128 MiB of HBM per device.

v0:
```python
import jax
import jax.numpy as jnp
from jax import lax
from jax.sharding import PartitionSpec as P

PATCH = 2048
NS_ITERS = 5
HIGH = lax.Precision.HIGHEST


def padded(block, sides, width):
    for axis, dim in sides:
        count = lax.axis_size(axis)
        forward = [(i, i + 1) for i in range(count - 1)]
        backward = [(target, source) for source, target in forward]
        low = lax.ppermute(
            lax.slice_in_dim(block, block.shape[dim] - width, None, axis=dim), axis, forward
        )
        high = lax.ppermute(lax.slice_in_dim(block, 0, width, axis=dim), axis, backward)
        block = jnp.concatenate([low, block, high], axis=dim)
    return block


def laplacian_update(haloed_ensemble, ensemble, spreading_factor, tendency_matrix):
    subdomain_lines = ensemble.shape[2]
    beside = jnp.pad(ensemble, ((0, 0), (0, 0), (0, 0), (1, 1)))
    laplace = (
        haloed_ensemble[:, :, 2:]
        + haloed_ensemble[:, :, :subdomain_lines]
        + beside[:, :, :, 2:]
        + beside[:, :, :, :-2]
        - 4.0 * ensemble
    )
    mixing = jnp.einsum("vw,kwxy->kvxy", tendency_matrix, ensemble, precision=HIGH)
    return ensemble + spreading_factor[None, :, None, None] * laplace + mixing


def transforms(gram, drive, member_count):
    identity_m = jnp.eye(member_count, dtype=jnp.float32)
    system = (member_count - 1.0) * identity_m + gram
    norm_value = jnp.sqrt(jnp.sum(system * system, axis=(-2, -1)))
    iterate = system / norm_value[..., None, None]
    inverse = jnp.broadcast_to(identity_m, system.shape)
    for sweep_no in range(NS_ITERS):
        middle = 1.5 * identity_m - 0.5 * jnp.einsum(
            "...ij,...jk->...ik", inverse, iterate, precision=HIGH
        )
        iterate = jnp.einsum("...ij,...jk->...ik", iterate, middle, precision=HIGH)
        inverse = jnp.einsum("...ij,...jk->...ik", middle, inverse, precision=HIGH)
    root = inverse / jnp.sqrt(norm_value)[..., None, None]
    inner = jnp.einsum("...ij,...j->...i", root, drive, precision=HIGH)
    offset = jnp.einsum("...ij,...j->...i", root, inner, precision=HIGH)
    return offset[..., :, None] + jnp.sqrt(member_count - 1.0) * root


def slot_ranks(patch_ids, patch_count):
    onehot = (patch_ids[..., None] == jnp.arange(patch_count, dtype=jnp.int32)).astype(jnp.int32)
    before = jnp.cumsum(onehot, axis=-2) - onehot
    return jnp.sum(before * onehot, axis=-1)


def shards(
    prior_ensemble,
    spreading_factor,
    tendency_matrix,
    measured_data,
    inverse_error,
    assigned_subregion,
    measured_entry,
    taper_index,
    taper_factors,
):
    ensemble_share, prognostic_number, subdomain_lines, eastward_span = prior_ensemble.shape
    groups = lax.axis_size("mem")
    members = ensemble_share * groups
    cells_dev = subdomain_lines * eastward_span // groups
    per_device = cells_dev // PATCH
    per_tile = per_device * groups
    haloed_ensemble = padded(prior_ensemble, (("dom", 2),), 1)
    advanced_ensemble = laplacian_update(
        haloed_ensemble, prior_ensemble, spreading_factor, tendency_matrix
    )
    moved = lax.all_to_all(
        advanced_ensemble.reshape(ensemble_share, prognostic_number, groups, cells_dev),
        "mem",
        split_axis=2,
        concat_axis=0,
        tiled=True,
    )
    ensemble = moved.reshape(members, prognostic_number, cells_dev)
    patch_ids = assigned_subregion.reshape(-1)
    obs_rows = patch_ids.shape[0]
    capacity = 2 * obs_rows // per_tile
    table_levels = taper_factors.shape[0]
    picks = (
        taper_index.reshape(-1)[:, None] == jnp.arange(table_levels, dtype=jnp.int32)[None, :]
    ).astype(jnp.float32)
    weight = inverse_error.reshape(-1) * jnp.dot(picks, taper_factors, precision=HIGH)
    values = measured_data.reshape(-1)
    columns = measured_entry.reshape(-1).astype(jnp.float32)
    target = patch_ids * capacity + slot_ranks(patch_ids, per_tile)

    def place_rows(field):
        return (
            jnp.zeros((per_tile * capacity,), jnp.float32)
            .at[target]
            .set(field)
            .reshape(groups, per_device * capacity)
        )

    received = (
        lax.all_to_all(place_rows(values), "mem", split_axis=0, concat_axis=0, tiled=True),
        lax.all_to_all(place_rows(weight), "mem", split_axis=0, concat_axis=0, tiled=True),
        lax.all_to_all(place_rows(columns), "mem", split_axis=0, concat_axis=0, tiled=True),
    )

    def arrange(field):
        return (
            field.reshape(groups, per_device, capacity)
            .transpose(1, 0, 2)
            .reshape(per_device, groups * capacity)
        )

    slot_value = arrange(received[0])
    slot_weight = arrange(received[1])
    slot_column = arrange(received[2])
    centre = jnp.mean(ensemble, axis=0)
    deviation = ensemble - centre[None]
    column_ids = slot_column.astype(jnp.int32)
    flat_index = (
        column_ids // PATCH * cells_dev
        + jnp.arange(per_device, dtype=jnp.int32)[:, None] * PATCH
        + column_ids % PATCH
    )
    flat_index = flat_index.reshape(-1)
    flat_dev = deviation.reshape(members, prognostic_number * cells_dev)
    obs_dev = jnp.take(flat_dev, flat_index, axis=1).reshape(members, per_device, -1)
    innovation = slot_value - jnp.take(centre.reshape(-1), flat_index).reshape(per_device, -1)
    weighted = obs_dev * slot_weight[None]
    gram = jnp.einsum("kps,jps->pkj", weighted, obs_dev, precision=HIGH)
    drive = jnp.einsum("kps,ps->pk", weighted, innovation, precision=HIGH)
    coeffs = transforms(gram, drive, members)
    dev_blocks = deviation.reshape(members, prognostic_number, per_device, PATCH)
    mixed = jnp.einsum("pjk,jvpt->kvpt", coeffs, dev_blocks, precision=HIGH)
    analysed = centre.reshape(1, prognostic_number, per_device, PATCH) + mixed
    outgoing = analysed.reshape(groups, ensemble_share, prognostic_number, cells_dev)
    returned = lax.all_to_all(outgoing, "mem", split_axis=0, concat_axis=3, tiled=True)
    return returned.reshape(ensemble_share, prognostic_number, subdomain_lines, eastward_span)


def solution(mesh):
    in_specs = (
        P("mem", None, "dom", None),
        P(),
        P(),
        P("dom", "mem"),
        P("dom", "mem"),
        P("dom", "mem", None),
        P("dom", "mem"),
        P("dom", "mem"),
        P(),
    )
    out_specs = P("mem", None, "dom", None)
    return jax.shard_map(shards, mesh=mesh, in_specs=in_specs, out_specs=out_specs, check_vma=False)
```

profile of v0, /device:TPU:0, one launch (start us, length us, event | category | flops | bytes accessed | tf_op | source)
XLA Modules:
  0.0 609.6 jit_solution(14362782641976846216)
XLA Ops:
  7.3 6.4 %all-to-all-start.1 = ((f32[8,1,128]{2,1,0:T(1,128)}), f32[8,1,128]{2,1,0:T(1,128)S(1)}, u32[]{:S(2)}, u32[]{:S(2)}) async-start(f32[8,1,128]{2,1,0:T(1,128)} %bitcast.14), calls=%async_computation.1 | async-start | bytes 8192 | tf_op jit(solution)/shard_map/all_to_all | solution.py:114
  16.3 4.7 collective-permute-start.1
  21.0 25.0 %fusion.8 = f32[8,128,512,4]{2,3,1,0:T(4,128)} fusion(f32[8,4,128,512]{3,2,1,0:T(8,128)} %param.9, f32[4,4]{1,0:T(4,128)S(1)} %copy-done), kind=kOutput, calls=%fused_computation.19 | convolution fusion | flops 100663296 | bytes 16777280 | tf_op jit(solution)/shard_map/vw,kwxy->kvxy/dot_general | solution.py:34
  49.1 5.1 all-to-all-start.3
  59.8 3.2 all-to-all-start.2
  63.1 22.8 %fusion.5 = f32[8,4,128,512]{3,2,1,0:T(8,128)} fusion(f32[8,4,128,512]{3,2,1,0:T(8,128)} %param.9, f32[8,4,1,512]{3,2,1,0:T(1,128)S(1)} %collective-permute-done.1, f32[8,4,1,512]{3,2,1,0:T(1,128)S(1)} %collective-permute-done, f32[8,128,512,4]{2,3,1,0:T(4,128)} %fusion.8, f32[4]{0:T(128)S(1)} %copy-done.3), kind=kLoop, calls=%fused_computation.12 | loop fusion | flops 20971520 | bytes 25296912 | tf_op jit(solution)/shard_map/add | solution.py:35
  85.9 9.4 %reshape.273 = f32[8,4,8,8192]{3,2,1,0:T(8,128)} reshape(f32[8,4,128,512]{3,2,1,0:T(8,128)} %fusion.5) | data formatting | bytes 16777216 | tf_op jit(solution)/shard_map/reshape | solution.py:84
  95.3 12.0 %copy.84 = f32[8,4,8,8192]{3,1,0,2:T(4,128)} copy(f32[8,4,8,8192]{3,2,1,0:T(8,128)} %reshape.273) | data formatting | bytes 16777216 | tf_op jit(solution)/shard_map/reshape | solution.py:84
  107.3 5.3 all-to-all-start
  115.2 181.3 %all-to-all-done = f32[8,4,8,8192]{3,1,0,2:T(4,128)} async-done(((f32[8,4,8,8192]{3,1,0,2:T(4,128)}), f32[8,4,8,8192]{3,1,0,2:T(4,128)}, u32[]{:S(2)}, u32[]{:S(2)}) %all-to-all-start) | async-done | bytes 8388640 | tf_op jit(solution)/shard_map/all_to_all | solution.py:83
  296.5 4.2 bitcast_reduce_fusion
  300.7 6.2 %gather_fusion.1 = f32[1024]{0:T(1024)S(1)} fusion(f32[32768]{0:T(1024)S(1)} %bitcast.131, s32[1024]{0:T(1024)S(1)} %broadcast_clamp_fusion), kind=kCustom, calls=%fused_computation.1 | custom fusion | bytes 12288 | tf_op jit(solution)/shard_map/jit(_take)/gather | solution.py:138
  306.9 8.1 %copy.111 = f32[8,8,4,8192]{3,1,2,0:T(8,128)S(1)} copy(f32[8,8,4,8192]{3,2,1,0:T(4,128)} %bitcast.56) | data formatting | bytes 16777216
  315.1 4.0 broadcast_subtract_fusion
  319.1 12.2 %copy.90 = f32[64,32768]{0,1:T(8,128)} copy(f32[64,32768]{1,0:T(8,128)} %broadcast_subtract_fusion) | data formatting | bytes 16777216 | tf_op jit(solution)/shard_map/sub | solution.py:128
  331.3 8.6 %gather_fusion = f32[1024,64]{1,0:T(8,128)S(1)} fusion(f32[64,32768]{0,1:T(8,128)} %copy.90, s32[1024]{0:T(1024)S(1)} %broadcast_clamp_fusion), kind=kCustom, calls=%fused_computation | custom fusion | bytes 528384 | tf_op jit(solution)/shard_map/jit(_take)/gather | solution.py:137
  345.5 12.1 %reshape.334 = f32[64,4,4,2048]{3,2,1,0:T(4,128)} reshape(f32[8,8,4,1,8192]{4,2,1,0,3:T(4,128)} %bitcast.4) | data formatting | bytes 16777216 | tf_op jit(solution)/shard_map/reshape | solution.py:90
  357.6 20.7 %bitcast_add_fusion = f32[64,4,4,2048]{3,0,1,2:T(8,128)} fusion(f32[64,4,4,2048]{3,2,1,0:T(4,128)} %reshape.334, f32[4,4,2048]{2,0,1:T(4,128)S(1)} %bitcast.136, f32[4,64,64]{2,1,0:T(8,128)S(1)} %convolution_divide_fusion, f32[4,64]{1,0:T(4,128)S(1)} %bitcast.140), kind=kOutput, calls=%fused_computation.16 | convolution fusion | flops 1614839808 | bytes 16974848 | tf_op jit(solution)/shard_map/pjk,jvpt->kvpt/dot_general | solution.py:144
  378.3 12.2 %copy.95 = f32[64,4,4,2048]{3,2,0,1:T(4,128)} copy(f32[64,4,4,2048]{3,0,1,2:T(8,128)} %bitcast_add_fusion) | data formatting | bytes 16777216 | tf_op jit(solution)/shard_map/add | solution.py:145
  390.5 10.9 %reshape.282 = f32[8,8,4,8192]{3,1,0,2:T(8,128)} reshape(f32[64,4,4,2048]{3,2,0,1:T(4,128)} %copy.95) | data formatting | bytes 16777216 | tf_op jit(solution)/shard_map/reshape | solution.py:146
  401.3 3.9 copy.96
  405.3 186.6 %all_to_all.57 = f32[8,8,4,8192]{3,1,2,0:T(8,128)S(1)} all-to-all(f32[8,8,4,8192]{3,1,2,0:T(8,128)S(1)} %copy.96), channel_id=1, replica_groups=mesh['mem'=8,'dom'=4] {'mem'}, dimensions={0} | all-to-all | bytes 16777216 | tf_op jit(solution)/shard_map/all_to_all | solution.py:147
  591.9 8.1 %copy.97 = f32[1,8,4,8,8192]{4,3,2,1,0:T(8,128)} copy(f32[1,8,4,8,8192]{4,1,2,3,0:T(8,128)S(1)} %bitcast.134) | data formatting | bytes 16777216 | tf_op jit(solution)/shard_map/all_to_all | solution.py:147
  600.0 9.4 %reshape.283 = f32[8,4,128,512]{3,2,1,0:T(8,128)} reshape(f32[1,8,4,8,8192]{4,3,2,1,0:T(8,128)} %copy.97) | data formatting | bytes 16777216 | tf_op jit(solution)/shard_map/reshape | solution.py:148
  (78 shorter events, 26.8 us)
Async XLA Ops:
  0.0 21.0 %copy-start = (f32[4,4]{1,0:T(4,128)S(1)}, f32[4,4]{1,0:T(4,128)}, u32[]{:S(2)}) copy-start(f32[4,4]{1,0:T(4,128)} %param.11) | copy-start | bytes 196
  7.3 41.9 %all-to-all-start.1 = ((f32[8,1,128]{2,1,0:T(1,128)}), f32[8,1,128]{2,1,0:T(1,128)S(1)}, u32[]{:S(2)}, u32[]{:S(2)}) async-start(f32[8,1,128]{2,1,0:T(1,128)} %bitcast.14), calls=%async_computation.1 | async-start | bytes 8192 | tf_op jit(solution)/shard_map/all_to_all | solution.py:114
  15.0 48.1 %collective-permute-start = (f32[8,4,1,512]{3,2,1,0:T(1,128)S(1)}, f32[8,4,1,512]{3,2,1,0:T(1,128)S(1)}, u32[]{:S(2)}, u32[]{:S(2)}) collective-permute-start(f32[8,4,1,512]{3,2,1,0:T(1,128)S(1)} %get-tuple-element.7), channel_id=1, source_target_pairs={{1,0},{2,1},{3,2},{5,4},{6,5},{7,6},{9,8},{10,9},{11,10},{13,12},{... | collective-permute-start | bytes 196616 | tf_op jit(solution)/shard_map/ppermute | solution.py:19
  16.3 38.0 %copy-start.4 = (s32[1,512]{1,0:T(1,128)S(1)}, s32[1,512]{1,0:T(1,128)}, u32[]{:S(2)}) copy-start(s32[1,512]{1,0:T(1,128)} %param.16) | copy-start | bytes 6148
  16.3 38.0 %copy-start.5 = (f32[64]{0:T(128)S(1)}, f32[64]{0:T(128)}, u32[]{:S(2)}) copy-start(f32[64]{0:T(128)} %param.17) | copy-start | bytes 772
  16.3 38.3 %copy-start.2 = (f32[1,512]{1,0:T(1,128)S(1)}, f32[1,512]{1,0:T(1,128)}, u32[]{:S(2)}) copy-start(f32[1,512]{1,0:T(1,128)} %param.13) | copy-start | bytes 6148
  16.3 46.8 %copy-start.3 = (f32[4]{0:T(128)S(1)}, f32[4]{0:T(128)}, u32[]{:S(2)}) copy-start(f32[4]{0:T(128)} %param.10) | copy-start | bytes 52
  16.3 46.8 %collective-permute-start.1 = (f32[8,4,1,512]{3,2,1,0:T(1,128)S(1)}, f32[8,4,1,512]{3,2,1,0:T(1,128)S(1)}, u32[]{:S(2)}, u32[]{:S(2)}) collective-permute-start(f32[8,4,1,512]{3,2,1,0:T(1,128)S(1)} %get-tuple-element.8), channel_id=1, source_target_pairs={{0,1},{1,2},{2,3},{4,5},{5,6},{6,7},{8,9},{9,10},{10,11},{12,13},{... | collective-permute-start | bytes 196616 | tf_op jit(solution)/shard_map/ppermute | solution.py:16
  49.1 10.7 %all-to-all-start.3 = ((f32[8,1,128]{2,1,0:T(1,128)}), f32[8,1,128]{2,1,0:T(1,128)S(1)}, u32[]{:S(2)}, u32[]{:S(2)}) async-start(f32[8,1,128]{2,1,0:T(1,128)} %bitcast.26), calls=%async_computation.3 | async-start | bytes 8192 | tf_op jit(solution)/shard_map/all_to_all | solution.py:112
  59.8 47.5 %all-to-all-start.2 = ((f32[8,1,128]{2,1,0:T(1,128)}), f32[8,1,128]{2,1,0:T(1,128)S(1)}, u32[]{:S(2)}, u32[]{:S(2)}) async-start(f32[8,1,128]{2,1,0:T(1,128)} %bitcast.23), calls=%async_computation.2 | async-start | bytes 8192 | tf_op jit(solution)/shard_map/all_to_all | solution.py:113
  107.3 189.2 %all-to-all-start = ((f32[8,4,8,8192]{3,1,0,2:T(4,128)}), f32[8,4,8,8192]{3,1,0,2:T(4,128)}, u32[]{:S(2)}, u32[]{:S(2)}) async-start(f32[8,4,8,8192]{3,1,0,2:T(4,128)} %copy.84), calls=%async_computation | async-start | bytes 16777216 | tf_op jit(solution)/shard_map/all_to_all | solution.py:83
  591.9 17.4 %copy-start.1 = (f32[4,4]{1,0:T(4,128)S(1)}, f32[4,4]{1,0:T(4,128)}, u32[]{:S(2)}) copy-start(f32[4,4]{1,0:T(4,128)} %param.11) | copy-start | bytes 196
where the time goes:
time: 621 us; the launch traced here: 610 us
  blocking collectives  187 us (30%)
  waiting for transfers between devices  183 us (29%)
  local copies, waits for them, and re-layouts  125 us (20%)
  matrix products  51.1 us (8%)
  other arithmetic  36.7 us (6%)
  starting transfers between devices  25.9 us (4%)
    all_to_all x1, blocking collectives, shards(): lax.all_to_all(outgoing, 'mem', split_axis=0, concat_axis=3, tiled=True)  187 us
    all_to_all x1, waiting for transfers between devices, shards(): lax.all_to_all(advanced_ensemble.reshape(ensemble_share, prognostic_numbe...  181 us
    dot_general x1, matrix products, laplacian_update(): jnp.einsum('vw,kwxy->kvxy', tendency_matrix, ensemble, precision=HIGH)  25 us
    add x1, other arithmetic, laplacian_update(): return ensemble + spreading_factor[None, :, None, None] * laplace + mixing  22.8 us
    reshape x2, local copies, waits for them, and re-layouts, shards(): advanced_ensemble.reshape(ensemble_share, prognostic_number, groups, cell...  21.3 us
    dot_general x1, matrix products, shards(): mixed = jnp.einsum('pjk,jvpt->kvpt', coeffs, dev_blocks, precision=HIGH)  20.7 us
    reshape x2, local copies, waits for them, and re-layouts, shards(): analysed.reshape(groups, ensemble_share, prognostic_number, cells_dev)  14.8 us
  transfers between devices with their start and end apart: 6, of which 2 were waited for; matrix products, arithmetic and copies ran while one was open for 13% of the time, Pallas kernels for 0%

commit v1 on v0

--- a/solution.py
+++ b/solution.py
@@ -144,7 +144,11 @@
     mixed = jnp.einsum("pjk,jvpt->kvpt", coeffs, dev_blocks, precision=HIGH)
     analysed = centre.reshape(1, prognostic_number, per_device, PATCH) + mixed
     outgoing = analysed.reshape(groups, ensemble_share, prognostic_number, cells_dev)
-    returned = lax.all_to_all(outgoing, "mem", split_axis=0, concat_axis=3, tiled=True)
+    parts_out = lax.psum(1, "mem")
+    shaped = jnp.split(outgoing, parts_out, axis=0)
+    w_next = jnp.stack(shaped)
+    arr_next = lax.all_to_all(w_next, "mem", 0, 0)
+    returned = jnp.concatenate(arr_next, axis=3)
     return returned.reshape(ensemble_share, prognostic_number, subdomain_lines, eastward_span)
 
 

time: 621 us -> 649 us (1.045)
  local copies, waits for them, and re-layouts: 125 us -> 153 us
    another operation x1 -> x11, local copies, waits for them, and re-layouts: 0.01 us -> 34.4 us  [the longest x9 25.1 us: shards(): w_next = jnp.stack(shaped)]
    split x0 -> x9, local copies, waits for them, and re-layouts: none -> 20.7 us  [shards(): shaped = jnp.split(outgoing, parts_out, axis=0)]
    reshape x3 -> x1, local copies, waits for them, and re-layouts: 24.2 us -> 8.08 us  [shards(): returned = jnp.concatenate(arr_next, axis=3)]
    add x1 -> x0, local copies, waits for them, and re-layouts: 12.2 us -> none  [shards(): analysed = centre.reshape(1, prognostic_number, per_device, PATCH) + mixed]
    unnamed x16 -> x35, local copies, waits for them, and re-layouts: 8.26 us -> 18 us
    all_to_all x1 -> x0, local copies, waits for them, and re-layouts: 8.08 us -> none  [shards(): lax.all_to_all(outgoing, 'mem', split_axis=0, concat_axis=3, tiled=True)]
  transfers between devices with their start and end apart: 6 -> 6, of which waited for: 2 -> 2; matrix products, arithmetic and copies ran while one was open for 13% -> 12% of each run, Pallas kernels for 0% -> 0%
where the time goes in v1:
time: 649 us; the launch traced here: 638 us
  blocking collectives  188 us (29%)
  waiting for transfers between devices  183 us (28%)
  local copies, waits for them, and re-layouts  153 us (24%)
  matrix products  49.4 us (8%)
  other arithmetic  36.7 us (6%)
  starting transfers between devices  26.1 us (4%)
    all_to_all x1, blocking collectives, shards(): arr_next = lax.all_to_all(w_next, 'mem', 0, 0)  188 us
    all_to_all x1, waiting for transfers between devices, shards(): lax.all_to_all(advanced_ensemble.reshape(ensemble_share, prognostic_numbe...  181 us
    another operation x9, local copies, waits for them, and re-layouts, shards(): w_next = jnp.stack(shaped)  25.1 us
    dot_general x1, matrix products, laplacian_update(): jnp.einsum('vw,kwxy->kvxy', tendency_matrix, ensemble, precision=HIGH)  25 us
    add x1, other arithmetic, laplacian_update(): return ensemble + spreading_factor[None, :, None, None] * laplace + mixing  22.8 us
    reshape x2, local copies, waits for them, and re-layouts, shards(): advanced_ensemble.reshape(ensemble_share, prognostic_number, groups, cell...  21.3 us
    split x9, local copies, waits for them, and re-layouts, shards(): shaped = jnp.split(outgoing, parts_out, axis=0)  20.7 us
    dot_general x1, matrix products, shards(): mixed = jnp.einsum('pjk,jvpt->kvpt', coeffs, dev_blocks, precision=HIGH)  19 us
  transfers between devices with their start and end apart: 6, of which 2 were waited for; matrix products, arithmetic and copies ran while one was open for 12% of the time, Pallas kernels for 0%

profile of v1, /device:TPU:0, one launch (start us, length us, event | category | flops | bytes accessed | tf_op | source)
XLA Modules:
  0.0 637.6 jit_solution(12470243655348502270)
XLA Ops:
  7.3 6.4 all-to-all-start.1
  16.3 4.7 collective-permute-start.1
  21.0 25.0 %fusion.8 = f32[8,128,512,4]{2,3,1,0:T(4,128)} fusion(f32[8,4,128,512]{3,2,1,0:T(8,128)} %param.9, f32[4,4]{1,0:T(4,128)S(1)} %copy-done), kind=kOutput, calls=%fused_computation.19 | convolution fusion | flops 100663296 | bytes 16777280 | tf_op jit(solution)/shard_map/vw,kwxy->kvxy/dot_general | solution.py:34
  46.0 3.2 scatter_custom_fusion.2
  49.1 5.1 all-to-all-start.3
  59.8 3.2 all-to-all-start.2
  63.1 22.8 %fusion.5 = f32[8,4,128,512]{3,2,1,0:T(8,128)} fusion(f32[8,4,128,512]{3,2,1,0:T(8,128)} %param.9, f32[8,4,1,512]{3,2,1,0:T(1,128)S(1)} %collective-permute-done.1, f32[8,4,1,512]{3,2,1,0:T(1,128)S(1)} %collective-permute-done, f32[8,128,512,4]{2,3,1,0:T(4,128)} %fusion.8, f32[4]{0:T(128)S(1)} %copy-done.9), kind=kLoop, calls=%fused_computation.12 | loop fusion | flops 20971520 | bytes 25296912 | tf_op jit(solution)/shard_map/add | solution.py:35
  85.9 9.4 %reshape.286 = f32[8,4,8,8192]{3,2,1,0:T(8,128)} reshape(f32[8,4,128,512]{3,2,1,0:T(8,128)} %fusion.5) | data formatting | bytes 16777216 | tf_op jit(solution)/shard_map/reshape | solution.py:84
  95.3 12.0 %copy.104 = f32[8,4,8,8192]{3,1,0,2:T(4,128)} copy(f32[8,4,8,8192]{3,2,1,0:T(8,128)} %reshape.286) | data formatting | bytes 16777216 | tf_op jit(solution)/shard_map/reshape | solution.py:84
  107.3 5.5 all-to-all-start
  115.4 181.3 %all-to-all-done = f32[8,4,8,8192]{3,1,0,2:T(4,128)} async-done(((f32[8,4,8,8192]{3,1,0,2:T(4,128)}), f32[8,4,8,8192]{3,1,0,2:T(4,128)}, u32[]{:S(2)}, u32[]{:S(2)}) %all-to-all-start) | async-done | bytes 8388640 | tf_op jit(solution)/shard_map/all_to_all | solution.py:83
  296.7 4.2 bitcast_reduce_fusion
  300.9 6.2 gather_fusion.1
  307.1 8.1 %copy.137 = f32[8,8,4,8192]{3,1,2,0:T(8,128)S(1)} copy(f32[8,8,4,8192]{3,2,1,0:T(4,128)} %bitcast.54) | data formatting | bytes 16777216
  315.2 4.0 broadcast_subtract_fusion
  319.3 12.2 %copy.110 = f32[64,32768]{0,1:T(8,128)} copy(f32[64,32768]{1,0:T(8,128)} %broadcast_subtract_fusion) | data formatting | bytes 16777216 | tf_op jit(solution)/shard_map/sub | solution.py:128
  331.5 8.6 %gather_fusion = f32[1024,64]{1,0:T(8,128)S(1)} fusion(f32[64,32768]{0,1:T(8,128)} %copy.110, s32[1024]{0:T(1024)S(1)} %broadcast_clamp_fusion), kind=kCustom, calls=%fused_computation | custom fusion | bytes 528384 | tf_op jit(solution)/shard_map/jit(_take)/gather | solution.py:137
  345.7 11.9 %reshape.346 = f32[64,4,4,2048]{3,2,1,0:T(4,128)} reshape(f32[8,8,4,1,8192]{4,2,1,0,3:T(4,128)} %bitcast.4) | data formatting | bytes 16777216 | tf_op jit(solution)/shard_map/reshape | solution.py:90
  357.6 19.0 %bitcast_add_fusion = f32[64,4,4,2048]{3,0,1,2:T(8,128)S(1)} fusion(f32[64,4,4,2048]{3,2,1,0:T(4,128)} %reshape.346, f32[4,4,2048]{2,0,1:T(4,128)S(1)} %bitcast.148, f32[4,64,64]{2,1,0:T(8,128)S(1)} %convolution_divide_fusion, f32[4,64]{1,0:T(4,128)S(1)} %bitcast.152), kind=kOutput, calls=%fused_computation.16 | convolution fusion | flops 1614839808 | bytes 16974848 | tf_op jit(solution)/shard_map/pjk,jvpt->kvpt/dot_general | solution.py:144
  415.5 3.0 stack.33
  420.2 3.3 stack.34
  432.0 187.6 %all_to_all.47 = f32[8,1,8,4,8192]{4,2,3,1,0:T(8,128)S(1)} all-to-all(f32[8,1,8,4,8192]{4,2,3,1,0:T(8,128)} %constant_dynamic-update-slice_fusion), channel_id=1, replica_groups=mesh['mem'=8,'dom'=4] {'mem'}, dimensions={0} | all-to-all | bytes 16777216 | tf_op jit(solution)/shard_map/all_to_all | solution.py:150
  619.7 8.1 %copy.123 = f32[1,8,4,8,8192]{4,3,2,1,0:T(8,128)} copy(f32[1,8,4,8,8192]{4,1,2,0,3:T(8,128)S(1)} %bitcast.146) | data formatting | bytes 16777216 | tf_op jit(solution)/shard_map/reshape | solution.py:151
  627.8 9.4 %reshape_reshape.3 = f32[8,4,128,512]{3,2,1,0:T(8,128)} reshape(f32[1,8,4,8,8192]{4,3,2,1,0:T(8,128)} %copy.123) | data formatting | bytes 16777216 | tf_op jit(solution)/shard_map/reshape;reshape | solution.py:152
  (112 shorter events, 72.7 us)
Async XLA Ops:
  0.0 21.0 %copy-start = (f32[4,4]{1,0:T(4,128)S(1)}, f32[4,4]{1,0:T(4,128)}, u32[]{:S(2)}) copy-start(f32[4,4]{1,0:T(4,128)} %param.11) | copy-start | bytes 196
  7.3 41.9 %all-to-all-start.1 = ((f32[8,1,128]{2,1,0:T(1,128)}), f32[8,1,128]{2,1,0:T(1,128)S(1)}, u32[]{:S(2)}, u32[]{:S(2)}) async-start(f32[8,1,128]{2,1,0:T(1,128)} %bitcast.14), calls=%async_computation.1 | async-start | bytes 8192 | tf_op jit(solution)/shard_map/all_to_all | solution.py:114
  15.0 48.1 %collective-permute-start = (f32[8,4,1,512]{3,2,1,0:T(1,128)S(1)}, f32[8,4,1,512]{3,2,1,0:T(1,128)S(1)}, u32[]{:S(2)}, u32[]{:S(2)}) collective-permute-start(f32[8,4,1,512]{3,2,1,0:T(1,128)S(1)} %get-tuple-element.15), channel_id=1, source_target_pairs={{1,0},{2,1},{3,2},{5,4},{6,5},{7,6},{9,8},{10,9},{11,10},{13,12},{... | collective-permute-start | bytes 196616 | tf_op jit(solution)/shard_map/ppermute | solution.py:19
  16.3 38.0 %copy-start.10 = (s32[1,512]{1,0:T(1,128)S(1)}, s32[1,512]{1,0:T(1,128)}, u32[]{:S(2)}) copy-start(s32[1,512]{1,0:T(1,128)} %param.16) | copy-start | bytes 6148
  16.3 38.0 %copy-start.11 = (f32[64]{0:T(128)S(1)}, f32[64]{0:T(128)}, u32[]{:S(2)}) copy-start(f32[64]{0:T(128)} %param.17) | copy-start | bytes 772
  16.3 38.3 %copy-start.8 = (f32[1,512]{1,0:T(1,128)S(1)}, f32[1,512]{1,0:T(1,128)}, u32[]{:S(2)}) copy-start(f32[1,512]{1,0:T(1,128)} %param.13) | copy-start | bytes 6148
  16.3 46.8 %copy-start.9 = (f32[4]{0:T(128)S(1)}, f32[4]{0:T(128)}, u32[]{:S(2)}) copy-start(f32[4]{0:T(128)} %param.10) | copy-start | bytes 52
  16.3 46.8 %collective-permute-start.1 = (f32[8,4,1,512]{3,2,1,0:T(1,128)S(1)}, f32[8,4,1,512]{3,2,1,0:T(1,128)S(1)}, u32[]{:S(2)}, u32[]{:S(2)}) collective-permute-start(f32[8,4,1,512]{3,2,1,0:T(1,128)S(1)} %get-tuple-element.16), channel_id=1, source_target_pairs={{0,1},{1,2},{2,3},{4,5},{5,6},{6,7},{8,9},{9,10},{10,11},{12,13},{... | collective-permute-start | bytes 196616 | tf_op jit(solution)/shard_map/ppermute | solution.py:16
  49.1 10.7 %all-to-all-start.3 = ((f32[8,1,128]{2,1,0:T(1,128)}), f32[8,1,128]{2,1,0:T(1,128)S(1)}, u32[]{:S(2)}, u32[]{:S(2)}) async-start(f32[8,1,128]{2,1,0:T(1,128)} %bitcast.26), calls=%async_computation.3 | async-start | bytes 8192 | tf_op jit(solution)/shard_map/all_to_all | solution.py:112
  59.8 47.5 %all-to-all-start.2 = ((f32[8,1,128]{2,1,0:T(1,128)}), f32[8,1,128]{2,1,0:T(1,128)S(1)}, u32[]{:S(2)}, u32[]{:S(2)}) async-start(f32[8,1,128]{2,1,0:T(1,128)} %bitcast.23), calls=%async_computation.2 | async-start | bytes 8192 | tf_op jit(solution)/shard_map/all_to_all | solution.py:113
  107.3 189.4 %all-to-all-start = ((f32[8,4,8,8192]{3,1,0,2:T(4,128)}), f32[8,4,8,8192]{3,1,0,2:T(4,128)}, u32[]{:S(2)}, u32[]{:S(2)}) async-start(f32[8,4,8,8192]{3,1,0,2:T(4,128)} %copy.104), calls=%async_computation | async-start | bytes 16777216 | tf_op jit(solution)/shard_map/all_to_all | solution.py:83
  410.8 12.7 %copy-start.2 = (f32[1,1,8,4,8192]{4,2,3,1,0:T(8,128)S(1)}, f32[1,1,8,4,8192]{4,2,3,1,0:T(8,128)}, u32[]{:S(2)}) copy-start(f32[1,1,8,4,8192]{4,2,3,1,0:T(8,128)} %stack.28) | copy-start | bytes 3145732
  415.5 9.0 %copy-start.3 = (f32[1,1,8,4,8192]{4,2,3,1,0:T(8,128)S(1)}, f32[1,1,8,4,8192]{4,2,3,1,0:T(8,128)}, u32[]{:S(2)}) copy-start(f32[1,1,8,4,8192]{4,2,3,1,0:T(8,128)} %stack.29) | copy-start | bytes 3145732
  420.2 7.6 %copy-start.4 = (f32[1,1,8,4,8192]{4,2,3,1,0:T(8,128)S(1)}, f32[1,1,8,4,8192]{4,2,3,1,0:T(8,128)}, u32[]{:S(2)}) copy-start(f32[1,1,8,4,8192]{4,2,3,1,0:T(8,128)} %stack.31) | copy-start | bytes 3145732
  423.5 5.4 copy-start.5
  423.5 6.4 %copy-start.6 = (f32[1,1,8,4,8192]{4,2,3,1,0:T(8,128)S(1)}, f32[1,1,8,4,8192]{4,2,3,1,0:T(8,128)}, u32[]{:S(2)}) copy-start(f32[1,1,8,4,8192]{4,2,3,1,0:T(8,128)} %stack.33) | copy-start | bytes 3145732
  423.5 7.5 %copy-start.7 = (f32[1,1,8,4,8192]{4,2,3,1,0:T(8,128)S(1)}, f32[1,1,8,4,8192]{4,2,3,1,0:T(8,128)}, u32[]{:S(2)}) copy-start(f32[1,1,8,4,8192]{4,2,3,1,0:T(8,128)} %stack.34) | copy-start | bytes 3145732
  619.7 17.4 %copy-start.1 = (f32[4,4]{1,0:T(4,128)S(1)}, f32[4,4]{1,0:T(4,128)}, u32[]{:S(2)}) copy-start(f32[4,4]{1,0:T(4,128)} %param.11) | copy-start | bytes 196
